TPU v7x, 256 devices: a whole 4x4x8 slice. The times are simulated.
256 devices in a mesh: row: 16 (over x, z_lo), col: 16 (over z_hi, y, core).
Axes of the slice: x: 4, y: 4, z: 8 (z_hi: 2, z_lo: 4; z = z_hi * 4 + z_lo), core: 2. Of those that a mesh axis runs over, the one named last changes fastest.
Arguments:
- acts: bfloat16 [2048, 5120], P('col', 'row'), may hold values from -60 to 60
- out_grads: bfloat16 [2048, 13824], P('row', 'col'), may hold values from -0.06187184 to 0.06187184
- momentum: float32 [5120, 13824], P('row', 'col'), may hold values from -200 to 200
- weight: float32 [5120, 13824], P('row', 'col'), may hold values from -0.078125 to 0.078125
Outputs:
- momentum_new: float32 [5120, 13824], P('row', 'col')
- update: bfloat16 [5120, 13824], P('row', 'col')
- weight_new: float32 [5120, 13824], P('row', 'col')
All inputs are finite; a program needn't handle non-finite values.
Results may differ from a plain program's by a relative error of at most 0.014.
Values may be sent and summed in bfloat16 or wider, within the bound.
A program may use at most 64 MiB of HBM per device.

v0:
```python
import math
import jax
import jax.numpy as jnp
from jax import lax
from jax.sharding import PartitionSpec as P

D = 5120


def body(acts, out_grads, momentum, weight):
    token_acts = lax.all_gather(acts, "col", axis=0, tiled=True)
    slab_rows = token_acts
    gradient = lax.dot_general(
        slab_rows,
        lax.all_gather(out_grads, "row", axis=0, tiled=True),
        (((0,), (0,)), ((), ())),
        preferred_element_type=jnp.float32,
    )
    momentum_new = 0.95 * momentum + gradient
    blended = gradient + 0.95 * momentum_new
    rounded = blended.astype(jnp.bfloat16)
    col_panel = lax.all_gather(rounded, "row", axis=0, tiled=True)
    slab_rows = col_panel
    gram_tile = lax.psum_scatter(
        lax.dot_general(
            slab_rows, rounded, (((1,), (1,)), ((), ())), preferred_element_type=jnp.float32
        ).astype(jnp.bfloat16),
        "col",
        scatter_dimension=0,
        tiled=True,
    )
    gram_cols = lax.all_gather(gram_tile, "col", axis=0, tiled=True)
    gram_rows = lax.all_gather(gram_tile, "row", axis=1, tiled=True)
    gram_square = jnp.dot(gram_rows, gram_cols, preferred_element_type=jnp.float32)
    total_sum = lax.psum(jnp.sum(gram_square * gram_square), ("row", "col"))
    schatten = jnp.sqrt(total_sum + 1e-06)
    square_root = jnp.sqrt(schatten)
    fourth_root = jnp.sqrt(square_root)
    poly_tile = (
        -4.775 * gram_tile.astype(jnp.float32) / square_root + 2.0315 * gram_square / schatten
    ).astype(jnp.bfloat16)
    poly_cols = lax.all_gather(poly_tile, "col", axis=0, tiled=True)
    product = lax.dot_general(
        poly_cols, col_panel, (((0,), (0,)), ((), ())), preferred_element_type=jnp.float32
    )
    orthogonal = (3.4445 * rounded.astype(jnp.float32) + product) / fourth_root
    factor = math.sqrt(D)
    update = (factor * orthogonal).astype(jnp.bfloat16)
    weight_new = 0.998 * weight - 0.02 * factor * orthogonal
    return (momentum_new, update, weight_new)


def solution(mesh):
    in_specs = (P("col", "row"), P("row", "col"), P("row", "col"), P("row", "col"))
    out_specs = (P("row", "col"), P("row", "col"), P("row", "col"))
    return jax.shard_map(body, mesh=mesh, in_specs=in_specs, out_specs=out_specs, check_vma=False)
```

profile of v0, /device:TPU:1, one launch (start us, length us, event | category | flops | bytes accessed | tf_op | source)
XLA Modules:
  0.0 829.8 jit_solution(14348969872725976175)
XLA Ops:
  7.2 0.0 all-gather.7.cloned.1.call-start
  7.2 0.7 all-gather.7.cloned.1.call-update
  7.9 0.0 all-gather.9.cloned.1.call-start
  7.9 0.7 all-gather.9.cloned.1.call-update
  8.6 0.0 all-gather.11.cloned.1.call-start
  8.7 63.7 %all-gather.7.cloned.1.call-done = bf16[2048,320]{0,1:T(8,128)(2,1)} async-done(((bf16[128,320]{0,1:T(8,128)(2,1)}), bf16[2048,320]{0,1:T(8,128)(2,1)}) %all-gather.7.cloned.1.call-update) | async-done | bytes 1310736 | tf_op jit(solution)/shard_map/all_gather | solution.py:11
  72.4 90.5 %all-gather.9.cloned.1.call-done = bf16[2048,864]{0,1:T(8,128)(2,1)} async-done(((bf16[128,864]{0,1:T(8,128)(2,1)}), bf16[2048,864]{0,1:T(8,128)(2,1)}) %all-gather.9.cloned.1.call-update) | async-done | bytes 3538960 | tf_op jit(solution)/shard_map/all_gather | solution.py:15
  162.9 5.5 add_convert_fusion
  168.4 0.0 all-gather.11.cloned.1.call-update
  168.4 0.0 reduce-scatter.2.cloned.1.call-start
  168.4 210.8 %all-gather.11.cloned.1.call-done = bf16[5120,864]{1,0:T(8,128)(2,1)} async-done(((bf16[320,864]{1,0:T(8,128)(2,1)}), bf16[5120,864]{1,0:T(8,128)(2,1)}) %all-gather.11.cloned.1.call-update) | async-done | bytes 8847376 | tf_op jit(solution)/shard_map/all_gather | solution.py:22
  379.3 9.3 %convolution_convert_fusion = bf16[5120,320]{1,0:T(8,128)(2,1)} fusion(bf16[5120,864]{1,0:T(8,128)(2,1)} %all-gather.11.cloned.1.call-done, bf16[320,864]{1,0:T(8,128)(2,1)} %get-tuple-element.3), kind=kOutput, calls=%fused_computation | convolution fusion | flops 2832793600 | bytes 12677120 | tf_op jit(solution)/shard_map/dot_general | solution.py:25
  388.5 0.0 reduce-scatter.2.cloned.1.call-update
  388.6 0.0 all-gather.15.cloned.1.call-start
  388.6 98.2 %reduce-scatter.2.cloned.1.call-done = bf16[320,320]{1,0:T(8,128)(2,1)} async-done(((bf16[5120,320]{1,0:T(8,128)(2,1)}), bf16[320,320]{1,0:T(8,128)(2,1)}) %reduce-scatter.2.cloned.1.call-update) | async-done | bytes 204816 | tf_op jit(solution)/shard_map/reduce_scatter | solution.py:24
  486.8 0.0 all-gather.15.cloned.1.call-update
  486.8 0.0 all-gather.13.cloned.1.call-start
  486.9 1.8 copy.7
  488.7 0.0 all-gather.13.cloned.1.call-update
  488.7 0.0 copy-start
  488.7 0.0 copy-start.1
  488.7 0.0 copy-start.2
  488.7 0.0 all-gather.17.cloned.1.call-start
  488.8 74.5 %all-gather.15.cloned.1.call-done = bf16[5120,320]{1,0:T(8,128)(2,1)} async-done(((bf16[320,320]{1,0:T(8,128)(2,1)}), bf16[5120,320]{1,0:T(8,128)(2,1)}) %all-gather.15.cloned.1.call-update) | async-done | bytes 3276816 | tf_op jit(solution)/shard_map/all_gather | solution.py:32
  563.2 93.3 %all-gather.13.cloned.1.call-done = bf16[320,5120]{0,1:T(8,128)(2,1)} async-done(((bf16[320,320]{0,1:T(8,128)(2,1)}), bf16[320,5120]{0,1:T(8,128)(2,1)}) %all-gather.13.cloned.1.call-update) | async-done | bytes 3276816 | tf_op jit(solution)/shard_map/all_gather | solution.py:33
  656.5 5.8 multiply_reduce_fusion
  662.3 77.1 %psum.7 = f32[]{:T(128)} all-reduce(f32[]{:T(128)} %get-tuple-element.7), channel_id=1, replica_groups=mesh['row'=16,'col'=16] {'row','col'}, use_global_device_ids=true, to_apply=%region_2.0 | all-reduce | flops 1 | bytes 8 | tf_op jit(solution)/shard_map/psum | solution.py:35
  740.2 0.0 copy-done
  740.2 0.8 add_convert_fusion.1
  741.0 0.0 all-gather.17.cloned.1.call-update
  741.1 72.2 %all-gather.17.cloned.1.call-done = bf16[5120,320]{1,0:T(8,128)(2,1)} async-done(((bf16[320,320]{1,0:T(8,128)(2,1)}), bf16[5120,320]{1,0:T(8,128)(2,1)}) %all-gather.17.cloned.1.call-update) | async-done | bytes 3276816 | tf_op jit(solution)/shard_map/all_gather | solution.py:42
  813.3 0.0 copy-done.1
  813.3 0.0 copy-done.2
  813.3 9.7 %multiply_subtract_fusion = (f32[320,864]{1,0:T(8,128)}, bf16[320,864]{1,0:T(8,128)(2,1)}) fusion(f32[320,864]{1,0:T(8,128)S(1)} %copy-done.2, f32[]{:T(128)S(6)} %sqrt.11, bf16[5120,320]{1,0:T(8,128)(2,1)} %all-gather.17.cloned.1.call-done, bf16[5120,864]{1,0:T(8,128)(2,1)} %all-gather.11.cloned.1.call-done, bf16[320,864]{1,0:T(8,128)(2,1)S(1)} %copy-done.1), kind=kOutput, calls=%fused_computation.3 | convolution fusion | flops 2833643520 | bytes 15441924 | tf_op jit(solution)/shard_map/dot_general | solution.py:43
Async XLA Ops:
  7.2 65.2 %all-gather.7.cloned.1.call-start = ((), (), s32[]{:S(2)}) async-start(), calls=%async_computation.1 | async-start | bytes 1392640 | tf_op jit(solution)/shard_map/all_gather | solution.py:11
  7.9 155.0 %all-gather.9.cloned.1.call-start = ((), (), s32[]{:S(2)}) async-start(), calls=%async_computation.2 | async-start | bytes 3760128 | tf_op jit(solution)/shard_map/all_gather | solution.py:15
  8.6 370.6 %all-gather.11.cloned.1.call-start = ((), (), s32[]{:S(2)}) async-start(), calls=%async_computation.3 | async-start | bytes 9748480 | tf_op jit(solution)/shard_map/all_gather | solution.py:22
  168.4 318.4 %reduce-scatter.2.cloned.1.call-start = ((), (), s32[]{:S(2)}) async-start(), calls=%async_computation.4 | async-start | bytes 4177920 | tf_op jit(solution)/shard_map/reduce_scatter | solution.py:24
  388.6 174.7 %all-gather.15.cloned.1.call-start = ((), (), s32[]{:S(2)}) async-start(), calls=%async_computation.6 | async-start | bytes 4177920 | tf_op jit(solution)/shard_map/all_gather | solution.py:32
  486.8 169.7 %all-gather.13.cloned.1.call-start = ((), (), s32[]{:S(2)}) async-start(), calls=%async_computation.5 | async-start | bytes 4177920 | tf_op jit(solution)/shard_map/all_gather | solution.py:33
  488.7 251.5 %copy-start = (bf16[320,320]{1,0:T(8,128)(2,1)S(1)}, bf16[320,320]{1,0:T(8,128)(2,1)}, u32[]{:S(2)}) copy-start(bf16[320,320]{1,0:T(8,128)(2,1)} %reduce-scatter.2.cloned.1.call-done) | copy-start | bytes 614404
  488.7 324.6 %copy-start.1 = (bf16[320,864]{1,0:T(8,128)(2,1)S(1)}, bf16[320,864]{1,0:T(8,128)(2,1)}, u32[]{:S(2)}) copy-start(bf16[320,864]{1,0:T(8,128)(2,1)} %get-tuple-element.3) | copy-start | bytes 1658884
  488.7 324.6 %copy-start.2 = (f32[320,864]{1,0:T(8,128)S(1)}, f32[320,864]{1,0:T(8,128)}, u32[]{:S(2)}) copy-start(f32[320,864]{1,0:T(8,128)} %param.7) | copy-start | bytes 3317764
  488.7 324.5 %all-gather.17.cloned.1.call-start = ((), (), s32[]{:S(2)}) async-start(), calls=%async_computation.7 | async-start | bytes 4177920 | tf_op jit(solution)/shard_map/all_gather | solution.py:42
Sparse Core Ops, SparseCore 0:
  10.5 61.8 all-gather.6
  74.1 88.7 all-gather.8
  168.5 210.7 all-gather.10
  388.7 98.0 reduce-scatter.1
  489.4 73.8 all-gather.14
  565.5 91.0 all-gather.12
  741.1 72.0 all-gather.16
where the time goes:
time: 830 us
  waiting for transfers between devices  705 us (85%)
  blocking collectives  77.1 us (9%)
  matrix products  30.3 us (4%)
  between operations  14.9 us (2%)
    all_gather x1, waiting for transfers between devices, body(): col_panel = lax.all_gather(rounded, 'row', axis=0, tiled=True)  211 us
    reduce_scatter x1, waiting for transfers between devices, body(): lax.psum_scatter(lax.dot_general(slab_rows, rounded, (((1,), (1,)), ((),...  98.2 us
    all_gather x1, waiting for transfers between devices, body(): gram_rows = lax.all_gather(gram_tile, 'row', axis=1, tiled=True)  93.3 us
    all_gather x1, waiting for transfers between devices, body(): lax.all_gather(out_grads, 'row', axis=0, tiled=True)  90.5 us
    psum x1, blocking collectives, body(): total_sum = lax.psum(jnp.sum(gram_square * gram_square), ('row', 'col'))  77.1 us
    all_gather x1, waiting for transfers between devices, body(): gram_cols = lax.all_gather(gram_tile, 'col', axis=0, tiled=True)  74.5 us
    all_gather x1, waiting for transfers between devices, body(): poly_cols = lax.all_gather(poly_tile, 'col', axis=0, tiled=True)  72.2 us
    all_gather x1, waiting for transfers between devices, body(): token_acts = lax.all_gather(acts, 'col', axis=0, tiled=True)  63.7 us
  transfers between devices with their start and end apart: 7, of which 7 were waited for; matrix products, arithmetic and copies ran while one was open for 0% of the time, Pallas kernels for 0%

commit v1 on v0

--- a/solution.py
+++ b/solution.py
@@ -29,7 +29,12 @@
         scatter_dimension=0,
         tiled=True,
     )
-    gram_cols = lax.all_gather(gram_tile, "col", axis=0, tiled=True)
+    gram_cols = jnp.concatenate(
+        lax.all_to_all(
+            jnp.stack([gram_tile for _ in range(lax.axis_size("col"))], axis=0), "col", 0, 0
+        ),
+        axis=0,
+    )
     gram_rows = lax.all_gather(gram_tile, "row", axis=1, tiled=True)
     gram_square = jnp.dot(gram_rows, gram_cols, preferred_element_type=jnp.float32)
     total_sum = lax.psum(jnp.sum(gram_square * gram_square), ("row", "col"))

time: 830 us -> 840 us (1.012)
    all_to_all x0 -> x1, waiting for transfers between devices: none -> 96.6 us  [body(): lax.all_to_all(jnp.stack([gram_tile for _ in range(lax.axis_size('col'))]...]
    all_gather x1 -> x0, waiting for transfers between devices: 74.5 us -> none  [body(): gram_cols = lax.all_gather(gram_tile, 'col', axis=0, tiled=True)]
    all_gather x1, waiting for transfers between devices: 93.3 us -> 67.6 us  [body(): gram_rows = lax.all_gather(gram_tile, 'row', axis=1, tiled=True)]
where the time goes in v1:
time: 840 us; the launch traced here: 839 us
  waiting for transfers between devices  700 us (83%)
  blocking collectives  82.2 us (10%)
  matrix products  30.4 us (4%)
  between operations  14.9 us (2%)
    all_gather x1, waiting for transfers between devices, body(): col_panel = lax.all_gather(rounded, 'row', axis=0, tiled=True)  211 us
    reduce_scatter x1, waiting for transfers between devices, body(): lax.psum_scatter(lax.dot_general(slab_rows, rounded, (((1,), (1,)), ((),...  98.2 us
    all_to_all x1, waiting for transfers between devices, body(): lax.all_to_all(jnp.stack([gram_tile for _ in range(lax.axis_size('col'))]...  96.6 us
    all_gather x1, waiting for transfers between devices, body(): lax.all_gather(out_grads, 'row', axis=0, tiled=True)  90.5 us
    psum x1, blocking collectives, body(): total_sum = lax.psum(jnp.sum(gram_square * gram_square), ('row', 'col'))  82.2 us
    all_gather x1, waiting for transfers between devices, body(): poly_cols = lax.all_gather(poly_tile, 'col', axis=0, tiled=True)  70.7 us
    all_gather x1, waiting for transfers between devices, body(): gram_rows = lax.all_gather(gram_tile, 'row', axis=1, tiled=True)  67.6 us
    all_gather x1, waiting for transfers between devices, body(): token_acts = lax.all_gather(acts, 'col', axis=0, tiled=True)  63.7 us
  transfers between devices with their start and end apart: 7, of which 7 were waited for; matrix products, arithmetic and copies ran while one was open for 0% of the time, Pallas kernels for 0%

profile of v1, /device:TPU:1, one launch (start us, length us, event | category | flops | bytes accessed | tf_op | source)
XLA Modules:
  0.0 839.5 jit_solution(12469018511275036384)
XLA Ops:
  7.2 0.0 all-gather.6.cloned.1.call-start
  7.2 0.7 all-gather.6.cloned.1.call-update
  7.9 0.0 all-gather.8.cloned.1.call-start
  7.9 0.7 all-gather.8.cloned.1.call-update
  8.6 0.0 all-gather.10.cloned.1.call-start
  8.7 63.7 %all-gather.6.cloned.1.call-done = bf16[2048,320]{0,1:T(8,128)(2,1)} async-done(((bf16[128,320]{0,1:T(8,128)(2,1)}), bf16[2048,320]{0,1:T(8,128)(2,1)}) %all-gather.6.cloned.1.call-update) | async-done | bytes 1310736 | tf_op jit(solution)/shard_map/all_gather | solution.py:11
  72.4 90.5 %all-gather.8.cloned.1.call-done = bf16[2048,864]{0,1:T(8,128)(2,1)} async-done(((bf16[128,864]{0,1:T(8,128)(2,1)}), bf16[2048,864]{0,1:T(8,128)(2,1)}) %all-gather.8.cloned.1.call-update) | async-done | bytes 3538960 | tf_op jit(solution)/shard_map/all_gather | solution.py:15
  162.9 5.5 add_convert_fusion
  168.4 0.0 all-gather.10.cloned.1.call-update
  168.4 0.0 reduce-scatter.2.cloned.1.call-start
  168.4 210.8 %all-gather.10.cloned.1.call-done = bf16[5120,864]{1,0:T(8,128)(2,1)} async-done(((bf16[320,864]{1,0:T(8,128)(2,1)}), bf16[5120,864]{1,0:T(8,128)(2,1)}) %all-gather.10.cloned.1.call-update) | async-done | bytes 8847376 | tf_op jit(solution)/shard_map/all_gather | solution.py:22
  379.3 9.2 %convolution_convert_fusion = bf16[5120,320]{1,0:T(8,128)(2,1)} fusion(bf16[5120,864]{1,0:T(8,128)(2,1)} %all-gather.10.cloned.1.call-done, bf16[320,864]{1,0:T(8,128)(2,1)} %get-tuple-element.3), kind=kOutput, calls=%fused_computation | convolution fusion | flops 2832793600 | bytes 12677120 | tf_op jit(solution)/shard_map/dot_general | solution.py:25
  388.5 0.0 reduce-scatter.2.cloned.1.call-update
  388.5 98.2 %reduce-scatter.2.cloned.1.call-done = bf16[320,320]{1,0:T(8,128)(2,1)} async-done(((bf16[5120,320]{1,0:T(8,128)(2,1)}), bf16[320,320]{1,0:T(8,128)(2,1)}) %reduce-scatter.2.cloned.1.call-update) | async-done | bytes 204816 | tf_op jit(solution)/shard_map/reduce_scatter | solution.py:24
  486.8 3.3 stack.2
  490.1 0.0 copy-start
  490.1 7.1 all-to-all-start
  497.2 0.0 all-gather.12.cloned.1.call-start
  497.3 0.0 copy-done
  497.3 0.9 copy.7
  498.2 0.0 all-gather.12.cloned.1.call-update
  498.2 0.0 all-gather.14.cloned.1.call-start
  498.2 96.6 %all-to-all-done = bf16[16,320,320]{2,1,0:T(8,128)(2,1)} async-done(((bf16[16,320,320]{2,1,0:T(8,128)(2,1)}), bf16[16,320,320]{2,1,0:T(8,128)(2,1)}, u32[]{:S(2)}, u32[]{:S(2)}) %all-to-all-start) | async-done | bytes 3276832 | tf_op jit(solution)/shard_map/all_to_all | solution.py:33
  594.9 67.6 %all-gather.12.cloned.1.call-done = bf16[320,5120]{0,1:T(8,128)(2,1)} async-done(((bf16[320,320]{0,1:T(8,128)(2,1)}), bf16[320,5120]{0,1:T(8,128)(2,1)}) %all-gather.12.cloned.1.call-update) | async-done | bytes 3276816 | tf_op jit(solution)/shard_map/all_gather | solution.py:38
  662.4 0.0 copy-start.1
  662.4 0.0 copy-start.2
  662.5 6.0 multiply_reduce_fusion
  668.4 82.2 %psum.7 = f32[]{:T(128)} all-reduce(f32[]{:T(128)} %get-tuple-element.7), channel_id=1, replica_groups=mesh['row'=16,'col'=16] {'row','col'}, use_global_device_ids=true, to_apply=%region_2.0 | all-reduce | flops 1 | bytes 8 | tf_op jit(solution)/shard_map/psum | solution.py:40
  751.3 0.8 add_convert_fusion.1
  752.1 0.0 all-gather.14.cloned.1.call-update
  752.2 70.7 %all-gather.14.cloned.1.call-done = bf16[5120,320]{1,0:T(8,128)(2,1)} async-done(((bf16[320,320]{1,0:T(8,128)(2,1)}), bf16[5120,320]{1,0:T(8,128)(2,1)}) %all-gather.14.cloned.1.call-update) | async-done | bytes 3276816 | tf_op jit(solution)/shard_map/all_gather | solution.py:47
  822.9 0.0 copy-done.1
  822.9 0.0 copy-done.2
  822.9 9.7 %multiply_subtract_fusion = (f32[320,864]{1,0:T(8,128)}, bf16[320,864]{1,0:T(8,128)(2,1)}) fusion(f32[320,864]{1,0:T(8,128)S(1)} %copy-done.2, f32[]{:T(128)S(6)} %sqrt.11, bf16[5120,320]{1,0:T(8,128)(2,1)} %all-gather.14.cloned.1.call-done, bf16[5120,864]{1,0:T(8,128)(2,1)} %all-gather.10.cloned.1.call-done, bf16[320,864]{1,0:T(8,128)(2,1)S(1)} %copy-done.1), kind=kOutput, calls=%fused_computation.3 | convolution fusion | flops 2833643520 | bytes 15441924 | tf_op jit(solution)/shard_map/dot_general | solution.py:48
Async XLA Ops:
  7.2 65.2 %all-gather.6.cloned.1.call-start = ((), (), s32[]{:S(2)}) async-start(), calls=%async_computation.2 | async-start | bytes 1392640 | tf_op jit(solution)/shard_map/all_gather | solution.py:11
  7.9 155.0 %all-gather.8.cloned.1.call-start = ((), (), s32[]{:S(2)}) async-start(), calls=%async_computation.3 | async-start | bytes 3760128 | tf_op jit(solution)/shard_map/all_gather | solution.py:15
  8.6 370.6 %all-gather.10.cloned.1.call-start = ((), (), s32[]{:S(2)}) async-start(), calls=%async_computation.4 | async-start | bytes 9748480 | tf_op jit(solution)/shard_map/all_gather | solution.py:22
  168.4 318.4 %reduce-scatter.2.cloned.1.call-start = ((), (), s32[]{:S(2)}) async-start(), calls=%async_computation.5 | async-start | bytes 4177920 | tf_op jit(solution)/shard_map/reduce_scatter | solution.py:24
  490.1 7.2 copy-start
  490.1 104.8 %all-to-all-start = ((bf16[16,320,320]{2,1,0:T(8,128)(2,1)}), bf16[16,320,320]{2,1,0:T(8,128)(2,1)}, u32[]{:S(2)}, u32[]{:S(2)}) async-start(bf16[16,320,320]{2,1,0:T(8,128)(2,1)} %stack.2), calls=%async_computation.1 | async-start | bytes 7864320 | tf_op jit(solution)/shard_map/all_to_all | solution.py:33
  497.2 165.2 %all-gather.12.cloned.1.call-start = ((), (), s32[]{:S(2)}) async-start(), calls=%async_computation.6 | async-start | bytes 4177920 | tf_op jit(solution)/shard_map/all_gather | solution.py:38
  498.2 324.7 %all-gather.14.cloned.1.call-start = ((), (), s32[]{:S(2)}) async-start(), calls=%async_computation.7 | async-start | bytes 4177920 | tf_op jit(solution)/shard_map/all_gather | solution.py:47
  662.4 160.5 %copy-start.1 = (bf16[320,864]{1,0:T(8,128)(2,1)S(1)}, bf16[320,864]{1,0:T(8,128)(2,1)}, u32[]{:S(2)}) copy-start(bf16[320,864]{1,0:T(8,128)(2,1)} %get-tuple-element.3) | copy-start | bytes 1658884
  662.4 160.5 %copy-start.2 = (f32[320,864]{1,0:T(8,128)S(1)}, f32[320,864]{1,0:T(8,128)}, u32[]{:S(2)}) copy-start(f32[320,864]{1,0:T(8,128)} %param.7) | copy-start | bytes 3317764
Sparse Core Ops, SparseCore 0:
  10.5 61.8 all-gather.5
  74.1 88.7 all-gather.7
  168.5 210.7 all-gather.9
  388.7 98.0 reduce-scatter.1
  500.1 162.2 all-gather.11
  752.3 70.5 all-gather.13
